TPU v7x, 512 devices: a whole 4x8x8 slice. The times are simulated.
512 devices in a mesh: row: 16 (over y, core), col: 32 (over z, x).
Axes of the slice: x: 4, y: 8, z: 8, core: 2. Of those that a mesh axis runs over, the one named last changes fastest.
Arguments:
- particles: float32 [16384, 128], P('row'), may hold values from -4 to 4
- log_weights: float32 [16384], P('row'), may hold values from -8 to 8
- targets: float32 [49152, 128], P('col'), may hold values from -5 to 5
Outputs:
- new_particles: float32 [49152, 128], P(('col', 'row'))
All inputs are finite; a program needn't handle non-finite values.
Results may differ from a plain program's by a relative error of at most 0.005.
Values sent between devices are 32-bit elements; how exact they have to be, the bound alone decides.
No kernel may reach another device: no remote copies, remote signals or barrier semaphores. Data moves between devices by JAX's collectives and lax.ppermute only.
A program may use at most 64 MiB of HBM per device.

v0:
```python
import math
import jax
import jax.numpy as jnp
from jax import lax
from jax.sharding import PartitionSpec as P

ITERS = 3
EPS = 0.01


def cost_tile(source, points):
    source_sq = jnp.sum(source * source, axis=1)
    points_sq = jnp.sum(points * points, axis=1)
    cross = jnp.dot(
        source, points.T, precision=lax.Precision.HIGHEST, preferred_element_type=jnp.float32
    )
    return (source_sq[:, None] + points_sq[None, :] - 2.0 * cross) / source.shape[1]


def row_update(particles, log_weights, targets, col_pot, block_count, block_rows):
    maxima = []
    totals = []
    for index in range(block_count):
        source = particles[index * block_rows : (index + 1) * block_rows]
        scores = (col_pot[None, :] - cost_tile(source, targets)) / EPS
        top = jnp.max(scores, axis=1)
        maxima.append(top)
        totals.append(jnp.sum(jnp.exp(scores - top[:, None]), axis=1))
    local_top = jnp.concatenate(maxima)
    local_sum = jnp.concatenate(totals)
    top = lax.pmax(local_top, "col")
    summed = lax.psum(local_sum * jnp.exp(local_top - top), "col")
    return EPS * (log_weights - (top + jnp.log(summed)))


def col_update(particles, targets, row_pot, block_count, block_rows):
    width = targets.shape[0]
    top = jnp.full((width,), -1e30, jnp.float32)
    summed = jnp.zeros((width,), jnp.float32)
    for index in range(block_count):
        source = particles[index * block_rows : (index + 1) * block_rows]
        potential = row_pot[index * block_rows : (index + 1) * block_rows]
        scores = (potential[:, None] - cost_tile(source, targets)) / EPS
        fresh = jnp.maximum(top, jnp.max(scores, axis=0))
        summed = summed * jnp.exp(top - fresh) + jnp.sum(jnp.exp(scores - fresh[None, :]), axis=0)
        top = fresh
    global_top = lax.pmax(top, "row")
    summed = lax.psum(summed * jnp.exp(top - global_top), "row")
    top = global_top
    return top + jnp.log(summed)


def per_device(particles, log_weights, targets):
    row_count = particles.shape[0]
    block_count = max(1, row_count // 512)
    block_rows = row_count // block_count
    log_count = math.log(targets.shape[0] * lax.axis_size("col"))
    col_pot = jnp.zeros((targets.shape[0],), jnp.float32)
    col_lse = col_pot
    row_pot = log_weights
    for iteration in range(ITERS):
        row_pot = row_update(particles, log_weights, targets, col_pot, block_count, block_rows)
        col_lse = col_update(particles, targets, row_pot, block_count, block_rows)
        col_pot = EPS * (-log_count - col_lse)
    particles_half = particles.astype(jnp.bfloat16)
    acc = jnp.zeros(
        (lax.axis_size("row") * (targets.shape[0] // lax.axis_size("row")), particles.shape[1]),
        jnp.float32,
    )
    for index in range(block_count):
        source = particles[index * block_rows : (index + 1) * block_rows]
        potential = row_pot[index * block_rows : (index + 1) * block_rows]
        plan = jnp.exp(
            (potential[:, None] - cost_tile(source, targets)) / EPS - col_lse[None, :]
        ).astype(jnp.bfloat16)
        source_half = particles_half[index * block_rows : (index + 1) * block_rows]
        acc = acc + lax.dot_general(
            plan, source_half, (((0,), (0,)), ((), ())), preferred_element_type=jnp.float32
        )
    return lax.psum_scatter(acc, "row", scatter_dimension=0, tiled=True)


def solution(mesh):
    placed = (P("row", None), P("row"), P("col", None))
    return jax.shard_map(
        per_device, mesh=mesh, in_specs=placed, out_specs=P(("col", "row"), None), check_vma=False
    )
```

profile of v0, /device:TPU:25, one launch (start us, length us, event | category | flops | bytes accessed | tf_op | source)
XLA Modules:
  0.0 693.4 jit_solution(18334036911586414496)
XLA Ops:
  6.5 0.0 reduce-scatter.2.cloned.1.call-start
  6.5 1.2 multiply_reduce_fusion.1
  7.8 1.1 convert_element_type.10
  8.9 0.0 copy-start.3
  8.9 0.0 copy-start.4
  8.9 1.5 multiply_reduce_fusion
  10.4 4.5 fusion.5
  14.9 0.0 copy-done.3
  14.9 0.0 copy-done.4
  14.9 4.8 fusion.4
  19.8 66.7 %pmax.42 = f32[1024]{0:T(1024)S(1)} all-reduce(f32[1024]{0:T(1024)S(1)} %pad_maximum_fusion), channel_id=1, replica_groups=mesh['row'=16,'col'=32] {'col'}, use_global_device_ids=true, to_apply=%region_5.0 | all-reduce | flops 1024 | bytes 8192 | tf_op jit(solution)/shard_map/pmax | solution.py:31
  86.4 0.0 copy-start.5
  86.4 3.2 exponential_reduce_fusion.10
  89.7 56.1 %psum.42 = f32[1024]{0:T(1024)S(1)} all-reduce(f32[1024]{0:T(1024)S(1)} %maximum_multiply_fusion), channel_id=1, replica_groups=mesh['row'=16,'col'=32] {'col'}, use_global_device_ids=true, to_apply=%region_8.0 | all-reduce | flops 1024 | bytes 8192 | tf_op jit(solution)/shard_map/psum | solution.py:32
  145.8 0.0 copy-done.5
  145.8 2.3 fusion.6
  148.1 0.4 fusion.7
  148.5 0.7 exponential_reduce_fusion.8
  149.2 51.3 %pmax.43 = f32[1536]{0:T(1024)S(1)} all-reduce(f32[1536]{0:T(1024)S(1)} %get-tuple-element.16), channel_id=1, replica_groups=mesh['row'=16,'col'=32] {'row'}, use_global_device_ids=true, to_apply=%region_11.0 | all-reduce | flops 1536 | bytes 12288 | tf_op jit(solution)/shard_map/pmax | solution.py:47
  200.5 2.6 exponential_reduce_fusion.9
  203.2 24.2 %psum.43 = f32[1536]{0:T(1024)S(1)} all-reduce(f32[1536]{0:T(1024)S(1)} %exponential_multiply_fusion.2), channel_id=1, replica_groups=mesh['row'=16,'col'=32] {'row'}, use_global_device_ids=true, to_apply=%region_14.0 | all-reduce | flops 1536 | bytes 12288 | tf_op jit(solution)/shard_map/psum | solution.py:48
  227.4 0.0 copy-start
  227.4 2.4 fusion.8
  229.9 0.4 copy-done
  230.3 1.0 exponential_reduce_fusion.7
  231.3 0.7 exponential_reduce_fusion.6
  232.0 57.4 %pmax.44 = f32[1024]{0:T(1024)S(1)} all-reduce(f32[1024]{0:T(1024)S(1)} %pad_maximum_fusion.1), channel_id=1, replica_groups=mesh['row'=16,'col'=32] {'col'}, use_global_device_ids=true, to_apply=%region_17.0 | all-reduce | flops 1024 | bytes 8192 | tf_op jit(solution)/shard_map/pmax | solution.py:31
  289.5 56.2 %psum.44 = f32[1024]{0:T(1024)S(1)} all-reduce(f32[1024]{0:T(1024)S(1)} %maximum_multiply_fusion.1), channel_id=1, replica_groups=mesh['row'=16,'col'=32] {'col'}, use_global_device_ids=true, to_apply=%region_20.0 | all-reduce | flops 1024 | bytes 8192 | tf_op jit(solution)/shard_map/psum | solution.py:32
  345.7 2.3 fusion.10
  348.0 0.4 fusion.11
  348.4 0.7 exponential_reduce_fusion.4
  349.1 51.7 %pmax.45 = f32[1536]{0:T(1024)S(1)} all-reduce(f32[1536]{0:T(1024)S(1)} %get-tuple-element.14), channel_id=1, replica_groups=mesh['row'=16,'col'=32] {'row'}, use_global_device_ids=true, to_apply=%region_23.0 | all-reduce | flops 1536 | bytes 12288 | tf_op jit(solution)/shard_map/pmax | solution.py:47
  400.8 2.6 exponential_reduce_fusion.5
  403.4 24.1 %psum.45 = f32[1536]{0:T(1024)S(1)} all-reduce(f32[1536]{0:T(1024)S(1)} %exponential_multiply_fusion.1), channel_id=1, replica_groups=mesh['row'=16,'col'=32] {'row'}, use_global_device_ids=true, to_apply=%region_26.0 | all-reduce | flops 1536 | bytes 12288 | tf_op jit(solution)/shard_map/psum | solution.py:48
  427.5 0.0 copy-start.1
  427.5 2.4 fusion.12
  429.9 0.4 copy-done.1
  430.3 1.0 exponential_reduce_fusion.3
  431.3 0.7 exponential_reduce_fusion.2
  432.1 57.4 %pmax.46 = f32[1024]{0:T(1024)S(1)} all-reduce(f32[1024]{0:T(1024)S(1)} %pad_maximum_fusion.2), channel_id=1, replica_groups=mesh['row'=16,'col'=32] {'col'}, use_global_device_ids=true, to_apply=%region_29.0 | all-reduce | flops 1024 | bytes 8192 | tf_op jit(solution)/shard_map/pmax | solution.py:31
  489.5 56.2 %psum.46 = f32[1024]{0:T(1024)S(1)} all-reduce(f32[1024]{0:T(1024)S(1)} %maximum_multiply_fusion.2), channel_id=1, replica_groups=mesh['row'=16,'col'=32] {'col'}, use_global_device_ids=true, to_apply=%region_32.0 | all-reduce | flops 1024 | bytes 8192 | tf_op jit(solution)/shard_map/psum | solution.py:32
  545.7 2.3 fusion.14
  548.0 0.4 fusion.15
  548.4 51.7 %pmax.47 = f32[1536]{0:T(1024)S(1)} all-reduce(f32[1536]{0:T(1024)S(1)} %get-tuple-element.12), channel_id=1, replica_groups=mesh['row'=16,'col'=32] {'row'}, use_global_device_ids=true, to_apply=%region_35.0 | all-reduce | flops 1536 | bytes 12288 | tf_op jit(solution)/shard_map/pmax | solution.py:47
  600.2 0.0 copy-start.2
  600.2 0.7 exponential_reduce_fusion
  600.9 1.2 copy-done.2
  602.0 0.7 exponential_reduce_fusion.1
  602.8 24.1 %psum.47 = f32[1536]{0:T(1024)S(1)} all-reduce(f32[1536]{0:T(1024)S(1)} %exponential_multiply_fusion), channel_id=1, replica_groups=mesh['row'=16,'col'=32] {'row'}, use_global_device_ids=true, to_apply=%region_38.0 | all-reduce | flops 1536 | bytes 12288 | tf_op jit(solution)/shard_map/psum | solution.py:48
  626.9 2.7 fusion.16
  629.6 1.8 convolution_add_fusion
  631.4 0.0 reduce-scatter.2.cloned.1.call-update
  631.4 55.2 %reduce-scatter.2.cloned.1.call-done = f32[96,128]{1,0:T(8,128)} async-done(((f32[1536,128]{1,0:T(8,128)}), f32[96,128]{1,0:T(8,128)}) %reduce-scatter.2.cloned.1.call-update) | async-done | bytes 49168 | tf_op jit(solution)/shard_map/reduce_scatter | solution.py:80
  (21 shorter events, 0.2 us)
Async XLA Ops:
  6.5 680.0 %reduce-scatter.2.cloned.1.call-start = ((), (), s32[]{:S(2)}) async-start(), calls=%async_computation.1 | async-start | bytes 835584 | tf_op jit(solution)/shard_map/reduce_scatter | solution.py:80
  8.9 6.0 copy-start.3
  8.9 6.0 copy-start.4
  86.4 59.4 %copy-start.5 = (f32[1024]{0:T(1024)S(1)}, f32[1024]{0:T(1024)}, u32[]{:S(2)}) copy-start(f32[1024]{0:T(1024)} %param.4) | copy-start | bytes 12292
  227.4 2.8 copy-start
  427.5 2.8 copy-start.1
  600.2 1.9 copy-start.2
Sparse Core Ops, SparseCore 0:
  631.5 54.9 reduce-scatter.1
where the time goes:
time: 694 us; the launch traced here: 693 us
  blocking collectives  577 us (83%)
  waiting for transfers between devices  55.2 us (8%)
  other arithmetic  31.5 us (5%)
  matrix products  13.8 us (2%)
  between operations  13.7 us (2%)
    pmax x3, blocking collectives, row_update(): top = lax.pmax(local_top, 'col')  182 us
    psum x3, blocking collectives, row_update(): summed = lax.psum(local_sum * jnp.exp(local_top - top), 'col')  168 us
    pmax x3, blocking collectives, col_update(): global_top = lax.pmax(top, 'row')  155 us
    psum x3, blocking collectives, col_update(): summed = lax.psum(summed * jnp.exp(top - global_top), 'row')  72.4 us
    reduce_scatter x1, waiting for transfers between devices, per_device(): return lax.psum_scatter(acc, 'row', scatter_dimension=0, tiled=True)  55.2 us
  transfers between devices with their start and end apart: 1, of which 1 were waited for; matrix products, arithmetic and copies ran while one was open for 0% of the time, Pallas kernels for 0%

commit v1 on v0

--- a/solution.py
+++ b/solution.py
@@ -45,7 +45,7 @@
         summed = summed * jnp.exp(top - fresh) + jnp.sum(jnp.exp(scores - fresh[None, :]), axis=0)
         top = fresh
     global_top = lax.pmax(top, "row")
-    summed = lax.psum(summed * jnp.exp(top - global_top), "row")
+    summed = jnp.sum(lax.all_gather(summed * jnp.exp(top - global_top), "row"), axis=0)
     top = global_top
     return top + jnp.log(summed)
 

time: 694 us -> 666 us (0.960)
  the two profiles are of different devices: /device:TPU:25 before, /device:TPU:29 now
where the time goes in v1:
time: 666 us; the launch traced here: 665 us
  blocking collectives  546 us (82%)
  waiting for transfers between devices  57.5 us (9%)
  other arithmetic  31.7 us (5%)
  matrix products  13.8 us (2%)
  between operations  13.7 us (2%)
    pmax x3, blocking collectives, row_update(): top = lax.pmax(local_top, 'col')  178 us
    psum x3, blocking collectives, row_update(): summed = lax.psum(local_sum * jnp.exp(local_top - top), 'col')  169 us
    pmax x3, blocking collectives, col_update(): global_top = lax.pmax(top, 'row')  149 us
    reduce_scatter x1, waiting for transfers between devices, per_device(): return lax.psum_scatter(acc, 'row', scatter_dimension=0, tiled=True)  57.5 us
    all_gather x3, blocking collectives, col_update(): lax.all_gather(summed * jnp.exp(top - global_top), 'row')  50.9 us
  transfers between devices with their start and end apart: 1, of which 1 were waited for; matrix products, arithmetic and copies ran while one was open for 0% of the time, Pallas kernels for 0%

profile of v1, /device:TPU:29, one launch (start us, length us, event | category | flops | bytes accessed | tf_op | source)
XLA Modules:
  0.0 665.2 jit_solution(1512242927766748921)
XLA Ops:
  6.5 0.0 reduce-scatter.2.cloned.1.call-start
  6.5 1.2 multiply_reduce_fusion.1
  7.8 1.1 convert_element_type.10
  8.9 0.0 copy-start.3
  8.9 0.0 copy-start.4
  8.9 1.5 multiply_reduce_fusion
  10.4 4.5 fusion.5
  14.9 0.0 copy-done.3
  14.9 0.0 copy-done.4
  14.9 4.8 fusion.4
  19.8 62.4 %pmax.42 = f32[1024]{0:T(1024)S(1)} all-reduce(f32[1024]{0:T(1024)S(1)} %pad_maximum_fusion), channel_id=1, replica_groups=mesh['row'=16,'col'=32] {'col'}, use_global_device_ids=true, to_apply=%region_5.0 | all-reduce | flops 1024 | bytes 8192 | tf_op jit(solution)/shard_map/pmax | solution.py:31
  82.1 0.0 copy-start.5
  82.1 3.2 exponential_reduce_fusion.10
  85.4 56.1 %psum.21 = f32[1024]{0:T(1024)S(1)} all-reduce(f32[1024]{0:T(1024)S(1)} %maximum_multiply_fusion), channel_id=1, replica_groups=mesh['row'=16,'col'=32] {'col'}, use_global_device_ids=true, to_apply=%region_8.0 | all-reduce | flops 1024 | bytes 8192 | tf_op jit(solution)/shard_map/psum | solution.py:32
  141.5 0.0 copy-done.5
  141.5 2.3 fusion.6
  143.8 0.4 fusion.7
  144.2 0.7 exponential_reduce_fusion.8
  144.9 51.3 %pmax.43 = f32[1536]{0:T(1024)S(1)} all-reduce(f32[1536]{0:T(1024)S(1)} %get-tuple-element.16), channel_id=1, replica_groups=mesh['row'=16,'col'=32] {'row'}, use_global_device_ids=true, to_apply=%region_11.0 | all-reduce | flops 1536 | bytes 12288 | tf_op jit(solution)/shard_map/pmax | solution.py:47
  196.3 2.6 exponential_reduce_fusion.9
  198.9 17.1 %all-gather.3 = f32[16,1,1536]{2,1,0:T(1,128)S(1)} all-gather(f32[1,1,1536]{2,1,0:T(1,128)S(1)} %reshape.45), channel_id=2, replica_groups=mesh['row'=16,'col'=32] {'row'}, dimensions={0}, use_global_device_ids=true | all-gather | bytes 104448 | tf_op jit(solution)/shard_map/all_gather | solution.py:48
  216.0 0.1 reduce_sum.169
  216.0 0.0 copy-start
  216.1 2.4 fusion.8
  218.5 0.4 copy-done
  218.9 1.0 exponential_reduce_fusion.7
  219.9 0.7 exponential_reduce_fusion.6
  220.7 57.7 %pmax.44 = f32[1024]{0:T(1024)S(1)} all-reduce(f32[1024]{0:T(1024)S(1)} %pad_maximum_fusion.1), channel_id=1, replica_groups=mesh['row'=16,'col'=32] {'col'}, use_global_device_ids=true, to_apply=%region_17.0 | all-reduce | flops 1024 | bytes 8192 | tf_op jit(solution)/shard_map/pmax | solution.py:31
  278.3 56.3 %psum.22 = f32[1024]{0:T(1024)S(1)} all-reduce(f32[1024]{0:T(1024)S(1)} %maximum_multiply_fusion.1), channel_id=1, replica_groups=mesh['row'=16,'col'=32] {'col'}, use_global_device_ids=true, to_apply=%region_20.0 | all-reduce | flops 1024 | bytes 8192 | tf_op jit(solution)/shard_map/psum | solution.py:32
  334.6 2.3 fusion.10
  336.9 0.4 fusion.11
  337.3 0.7 exponential_reduce_fusion.4
  338.0 48.9 %pmax.45 = f32[1536]{0:T(1024)S(1)} all-reduce(f32[1536]{0:T(1024)S(1)} %get-tuple-element.14), channel_id=1, replica_groups=mesh['row'=16,'col'=32] {'row'}, use_global_device_ids=true, to_apply=%region_23.0 | all-reduce | flops 1536 | bytes 12288 | tf_op jit(solution)/shard_map/pmax | solution.py:47
  386.9 2.6 exponential_reduce_fusion.5
  389.6 16.9 %all-gather.4 = f32[16,1,1536]{2,1,0:T(1,128)S(1)} all-gather(f32[1,1,1536]{2,1,0:T(1,128)S(1)} %reshape.47), channel_id=3, replica_groups=mesh['row'=16,'col'=32] {'row'}, dimensions={0}, use_global_device_ids=true | all-gather | bytes 104448 | tf_op jit(solution)/shard_map/all_gather | solution.py:48
  406.5 0.1 reduce_sum.177
  406.5 0.0 copy-start.1
  406.6 2.4 fusion.12
  409.0 0.4 copy-done.1
  409.4 1.0 exponential_reduce_fusion.3
  410.4 0.7 exponential_reduce_fusion.2
  411.1 57.7 %pmax.46 = f32[1024]{0:T(1024)S(1)} all-reduce(f32[1024]{0:T(1024)S(1)} %pad_maximum_fusion.2), channel_id=1, replica_groups=mesh['row'=16,'col'=32] {'col'}, use_global_device_ids=true, to_apply=%region_29.0 | all-reduce | flops 1024 | bytes 8192 | tf_op jit(solution)/shard_map/pmax | solution.py:31
  468.9 56.2 %psum.23 = f32[1024]{0:T(1024)S(1)} all-reduce(f32[1024]{0:T(1024)S(1)} %maximum_multiply_fusion.2), channel_id=1, replica_groups=mesh['row'=16,'col'=32] {'col'}, use_global_device_ids=true, to_apply=%region_32.0 | all-reduce | flops 1024 | bytes 8192 | tf_op jit(solution)/shard_map/psum | solution.py:32
  525.1 2.3 fusion.14
  527.4 0.4 fusion.15
  527.8 48.9 %pmax.47 = f32[1536]{0:T(1024)S(1)} all-reduce(f32[1536]{0:T(1024)S(1)} %get-tuple-element.12), channel_id=1, replica_groups=mesh['row'=16,'col'=32] {'row'}, use_global_device_ids=true, to_apply=%region_35.0 | all-reduce | flops 1536 | bytes 12288 | tf_op jit(solution)/shard_map/pmax | solution.py:47
  576.8 0.0 copy-start.2
  576.8 0.7 exponential_reduce_fusion
  577.5 1.2 copy-done.2
  578.6 0.7 exponential_reduce_fusion.1
  579.4 16.9 %all-gather.5 = f32[16,1,1536]{2,1,0:T(1,128)S(1)} all-gather(f32[1,1,1536]{2,1,0:T(1,128)S(1)} %reshape.49), channel_id=4, replica_groups=mesh['row'=16,'col'=32] {'row'}, dimensions={0}, use_global_device_ids=true | all-gather | bytes 104448 | tf_op jit(solution)/shard_map/all_gather | solution.py:48
  596.3 0.1 reduce_sum.188
  596.4 2.7 fusion.16
  599.1 1.8 convolution_add_fusion
  600.9 0.0 reduce-scatter.2.cloned.1.call-update
  600.9 57.5 %reduce-scatter.2.cloned.1.call-done = f32[96,128]{1,0:T(8,128)} async-done(((f32[1536,128]{1,0:T(8,128)}), f32[96,128]{1,0:T(8,128)}) %reduce-scatter.2.cloned.1.call-update) | async-done | bytes 49168 | tf_op jit(solution)/shard_map/reduce_scatter | solution.py:80
  (24 shorter events, 0.2 us)
Async XLA Ops:
  6.5 651.8 %reduce-scatter.2.cloned.1.call-start = ((), (), s32[]{:S(2)}) async-start(), calls=%async_computation.1 | async-start | bytes 835584 | tf_op jit(solution)/shard_map/reduce_scatter | solution.py:80
  8.9 6.0 copy-start.3
  8.9 6.0 copy-start.4
  82.1 59.4 %copy-start.5 = (f32[1024]{0:T(1024)S(1)}, f32[1024]{0:T(1024)}, u32[]{:S(2)}) copy-start(f32[1024]{0:T(1024)} %param.4) | copy-start | bytes 12292
  216.0 2.8 copy-start
  406.5 2.8 copy-start.1
  576.8 1.9 copy-start.2
Sparse Core Ops, SparseCore 0:
  601.0 57.2 reduce-scatter.1
